TPU v7x, 32 devices: a whole 2x2x4 slice. The times are simulated.
32 devices in a mesh: req: 8 (over z, x), grp: 4 (over y, core).
Axes of the slice: x: 2, y: 2, z: 4, core: 2. Of those that a mesh axis runs over, the one named last changes fastest.
Arguments:
- hidden: bfloat16 [256, 16, 1024], P(('grp', 'req')), parts along dimension 0, may hold values from -6 to 6
- norm_gain: float32 [1024], replicated, may hold values from 0.1 to 1.9
- in_weight: bfloat16 [1024, 4096], replicated, may hold values from -0.1875 to 0.1875
- conv_weight: float32 [4, 2048], P(None, 'req'), may hold values from -3 to 3
- conv_bias: float32 [2048], P('req'), may hold values from -3 to 3
- x_weight: bfloat16 [2048, 160], P('req'), may hold values from -0.125 to 0.125
- step_weight: bfloat16 [128, 2048], P(None, 'req'), may hold values from -0.5 to 0.5
- step_bias: float32 [2048], P('req'), may hold values from -5 to -1
- log_decay: float32 [16, 2048], P(None, 'req'), may hold values from -0.7 to 2.8
- skip_gain: float32 [2048], P('req'), may hold values from 0.5 to 1.5
- out_weight: bfloat16 [2048, 1024], replicated, may hold values from -0.125 to 0.125
- old_states: float32 [256, 16, 2048], P(('grp', 'req')), parts along dimension 0, may hold values from -3 to 3
- old_edges: bfloat16 [256, 3, 2048], P(('grp', 'req')), parts along dimension 0, may hold values from -6 to 6
- anchor: int32 [256], P('grp'), parts along dimension 0, may hold values from 0 to 63, each once
- fresh_flag: int32 [256], P('grp'), parts along dimension 0, may hold values 0 or 1
- accepted: int32 [256], P('grp'), parts along dimension 0, may hold values from 1 to 16
- request_ages: int32 [256], P('grp'), parts along dimension 0, may hold values from 0 to 7
Outputs:
- layer_out: bfloat16 [256, 16, 1024], P(('grp', 'req')), parts along dimension 0
- new_states: float32 [256, 16, 2048], P(('grp', 'req')), parts along dimension 0
There are 4 independent parts, one for each index of `grp`. A program takes and returns all parts, laid end to end along the dimension named above; an argument that names none is the same for every part. Nothing has to cross between parts.
Inputs may be any that keep to these rules, and one draw needn't show every extreme that they name: Every old slot is the anchor of exactly one request.
All inputs are finite; a program needn't handle non-finite values.
Results may differ from a plain program's by a relative error of at most 0.0091.
Values may be sent and summed in bfloat16 or wider, within the bound.
No kernel may reach another device: no remote copies, remote signals or barrier semaphores. Data moves between devices by JAX's collectives and lax.ppermute only.
A program may use at most 128 MiB of HBM per device.

v0:
```python
import jax
import jax.numpy as jnp
from jax import lax
from jax.sharding import PartitionSpec as P

EPS = 1e-05


def rms_normed(values_in, norm_gain):
    values = values_in.astype(jnp.float32)
    factor = lax.rsqrt(jnp.mean(values * values, axis=-1, keepdims=True) + EPS)
    return (values * factor * norm_gain).astype(jnp.bfloat16)


def on_device(
    hidden,
    norm_gain,
    in_weight,
    conv_weight,
    conv_bias,
    x_weight,
    step_weight,
    step_bias,
    log_decay,
    skip_gain,
    out_weight,
    old_states,
    old_edges,
    anchor,
    fresh_flag,
    accepted,
    request_ages,
):
    local_reqs, draft_len, width = hidden.shape
    inner_width = out_weight.shape[0]
    channels = conv_weight.shape[1]
    state_size = log_decay.shape[0]
    low_rank = step_weight.shape[0]
    span = old_edges.shape[1]
    state_lead = jnp.swapaxes(old_states, 0, 1)
    edge_lead = jnp.swapaxes(old_edges.astype(jnp.float32), 0, 1)
    moved_states, moved_edges = (
        lax.all_to_all(state_lead, "req", split_axis=2, concat_axis=1, tiled=True),
        lax.all_to_all(edge_lead, "req", split_axis=2, concat_axis=1, tiled=True),
    )
    token_major = jnp.swapaxes(hidden, 0, 1).reshape(draft_len * local_reqs, width)
    normed = rms_normed(token_major, norm_gain)
    projected = jnp.dot(normed, in_weight, preferred_element_type=jnp.float32).astype(jnp.bfloat16)
    projected = jnp.moveaxis(projected.reshape(draft_len, local_reqs, 2, inner_width), 2, 0)
    grouped = lax.all_to_all(projected, "req", split_axis=3, concat_axis=2, tiled=True)
    all_reqs = grouped.shape[2]
    inner_part = grouped[0]
    gate_part = grouped[1]
    keep_state = (1 - fresh_flag).astype(jnp.float32)
    start_state = jnp.take(moved_states, anchor, axis=1) * keep_state[None, :, None]
    edges = jnp.take(moved_edges, anchor, axis=1)
    distance = span - jnp.arange(span, dtype=jnp.int32)
    usable = (distance[:, None] <= request_ages[None, :]) & (fresh_flag[None, :] == 0)
    history = jnp.where(usable[:, :, None], edges, jnp.zeros((), jnp.float32))
    sequence = jnp.concatenate([history, inner_part.astype(jnp.float32)], axis=0)
    running = conv_bias + conv_weight[0] * sequence[0:draft_len]
    for offset in range(1, conv_weight.shape[0]):
        running = running + conv_weight[offset] * sequence[offset : offset + draft_len]
    conv_out = jax.nn.silu(running).astype(jnp.bfloat16)
    conv_rows = conv_out.reshape(draft_len * all_reqs, channels)
    partial_value = jnp.dot(conv_rows, x_weight, preferred_element_type=jnp.float32)
    mixed_rows = lax.psum(partial_value, "req").astype(jnp.bfloat16)
    flat = all_reqs * channels
    step_sizes = jax.nn.softplus(
        jnp.dot(mixed_rows[:, :low_rank], step_weight, preferred_element_type=jnp.float32)
        + step_bias
    )
    step_sizes = step_sizes.reshape(draft_len, flat)
    coeffs = (
        mixed_rows[:, low_rank:].astype(jnp.float32).reshape(draft_len, all_reqs, 2 * state_size)
    )
    b_coeff = coeffs[:, :, :state_size]
    c_coeff = coeffs[:, :, state_size:]
    inputs = conv_out.astype(jnp.float32)
    flat_inputs = inputs.reshape(draft_len, flat)
    decay = jnp.broadcast_to(
        (-jnp.exp(log_decay))[:, None, :], (state_size, all_reqs, channels)
    ).reshape(state_size, flat)
    start_flat = start_state.reshape(state_size, flat)

    def spread(per_token):
        return jnp.broadcast_to(
            jnp.swapaxes(per_token, 0, 1)[:, :, None], (state_size, all_reqs, channels)
        ).reshape(state_size, flat)

    def advance(carried, sliced):
        current, chosen = carried
        step_delta, step_b, step_c, step_input, step_index = sliced
        factor = jnp.exp(step_delta[None, :] * decay)
        current = factor * current + (step_delta * step_input)[None, :] * spread(step_b)
        result = jnp.sum(spread(step_c) * current, axis=0)
        picked = jnp.broadcast_to(
            (accepted == step_index + 1)[:, None], (all_reqs, channels)
        ).reshape(flat)
        chosen = jnp.where(picked[None, :], current, chosen)
        return ((current, chosen), result)

    sliced = (step_sizes, b_coeff, c_coeff, flat_inputs, jnp.arange(draft_len, dtype=jnp.int32))
    (final_state, chosen), outputs = lax.scan(advance, (start_flat, start_flat), sliced)
    outputs = outputs.reshape(draft_len, all_reqs, channels)
    gated_rows = (
        (outputs + skip_gain * inputs) * jax.nn.silu(gate_part.astype(jnp.float32))
    ).astype(jnp.bfloat16)
    returned = lax.all_to_all(gated_rows, "req", split_axis=1, concat_axis=2, tiled=True)
    layer_out = jnp.dot(
        returned.reshape(draft_len * local_reqs, inner_width),
        out_weight,
        preferred_element_type=jnp.float32,
    ).astype(jnp.bfloat16)
    layer_out = jnp.swapaxes(layer_out.reshape(draft_len, local_reqs, width), 0, 1)
    owned = lax.all_to_all(
        chosen.reshape(state_size, all_reqs, channels),
        "req",
        split_axis=1,
        concat_axis=2,
        tiled=True,
    )
    return (layer_out, jnp.swapaxes(owned, 0, 1))


def solution(mesh):
    return jax.shard_map(
        on_device,
        mesh=mesh,
        in_specs=(
            P(("grp", "req"), None, None),
            P(),
            P(),
            P(None, "req"),
            P("req"),
            P("req", None),
            P(None, "req"),
            P("req"),
            P(None, "req"),
            P("req"),
            P(),
            P(("grp", "req"), None, None),
            P(("grp", "req"), None, None),
            P("grp"),
            P("grp"),
            P("grp"),
            P("grp"),
        ),
        out_specs=(P(("grp", "req"), None, None), P(("grp", "req"), None, None)),
        check_vma=False,
    )
```

profile of v0, /device:TPU:0, one launch (start us, length us, event | category | flops | bytes accessed | tf_op | source)
XLA Modules:
  0.0 369.8 jit_solution(14479661632174473123)
XLA Ops:
  0.7 4.0 %copy.100 = f32[8,3,2048]{0,1,2:T(4,128)} copy(bf16[8,3,2048]{2,0,1:T(8,128)(2,1)} %param.31) | data formatting | bytes 294912 | tf_op jit(solution)/shard_map/transpose | solution.py:41
  4.7 3.9 %bitcast_bitcast_fusion.2 = f32[2048,3,8]{2,1,0:T(4,128)} fusion(f32[8,3,2048]{0,1,2:T(4,128)} %copy.100), kind=kLoop, calls=%fused_computation.72 | loop fusion | bytes 393216
  8.6 5.1 %reshape.188 = f32[8,1,6144]{2,1,0:T(1,128)} reshape(f32[2048,3,8]{2,1,0:T(4,128)} %bitcast_bitcast_fusion.2) | data formatting | bytes 393216
  13.7 7.3 %all-to-all-start.1 = ((f32[8,1,6144]{2,1,0:T(1,128)}), f32[8,1,6144]{2,1,0:T(1,128)S(1)}, u32[]{:S(2)}, u32[]{:S(2)}) async-start(f32[8,1,6144]{2,1,0:T(1,128)} %reshape.188), calls=%async_computation.1 | async-start | bytes 393216 | tf_op jit(solution)/shard_map/all_to_all | solution.py:44
  20.9 4.7 %copy.94 = f32[8,16,2048]{1,0,2:T(8,128)} copy(f32[8,16,2048]{2,1,0:T(8,128)S(1)} %copy-done.3) | data formatting | bytes 2097152 | tf_op args[11]
  26.0 4.8 %convolution_convert_fusion = bf16[128,4096]{1,0:T(8,128)(2,1)S(1)} fusion(bf16[1024,4096]{1,0:T(8,128)(2,1)} %param.21, f32[1024]{0:T(1024)S(1)} %copy-done.4, f32[128]{0:T(128)S(1)} %rsqrt.12, bf16[8,16,1024]{2,1,0:T(8,128)(2,1)S(1)} %copy-done.2), kind=kOutput, calls=%fused_computation.11 | convolution fusion | flops 1074790400 | bytes 9703936 | tf_op jit(solution)/shard_map/dot_general | solution.py:48
  30.8 8.9 %copy.103 = bf16[16,8,2,2048]{0,1,2,3:T(8,128)(2,1)} copy(bf16[16,8,2,2048]{3,1,2,0:T(8,128)(2,1)S(1)} %bitcast.169) | data formatting | bytes 2097152 | tf_op jit(solution)/shard_map/reshape | solution.py:49
  39.6 7.5 %bitcast_bitcast_fusion = bf16[2048,2,8,16]{3,2,1,0:T(8,128)(2,1)} fusion(bf16[16,8,2,2048]{0,1,2,3:T(8,128)(2,1)} %copy.103), kind=kLoop, calls=%fused_computation.70 | loop fusion | bytes 2097152
  47.1 5.8 %bitcast_bitcast_fusion.1 = f32[2048,8,16]{2,1,0:T(8,128)} fusion(f32[8,16,2048]{1,0,2:T(8,128)} %copy.94), kind=kLoop, calls=%fused_computation.71 | loop fusion | bytes 2097152
  52.9 8.1 %reshape.184 = f32[8,1,32768]{2,1,0:T(1,128)} reshape(f32[2048,8,16]{2,1,0:T(8,128)} %bitcast_bitcast_fusion.1) | data formatting | bytes 2097152
  61.1 6.0 %all-to-all-start = ((f32[8,1,32768]{2,1,0:T(1,128)}), f32[8,1,32768]{2,1,0:T(1,128)S(1)}, u32[]{:S(2)}, u32[]{:S(2)}) async-start(f32[8,1,32768]{2,1,0:T(1,128)} %reshape.184), calls=%async_computation | async-start | bytes 2097152 | tf_op jit(solution)/shard_map/all_to_all | solution.py:43
  67.3 11.3 %reshape.186 = bf16[8,2,32768]{2,1,0:T(2,128)(2,1)} reshape(bf16[2048,2,8,16]{3,2,1,0:T(8,128)(2,1)} %bitcast_bitcast_fusion) | data formatting | bytes 2097152
  80.5 4.7 %reshape.189 = f32[2048,3,8]{2,1,0:T(4,128)} reshape(f32[8,6144]{1,0:T(8,128)S(1)} %reduce.3) | data formatting | bytes 393216
  85.2 3.5 copy.101
  89.6 2.9 all-to-all-done
  92.5 3.7 %all-to-all-start.2 = ((bf16[8,2,32768]{2,1,0:T(2,128)(2,1)}), bf16[8,2,32768]{2,1,0:T(2,128)(2,1)S(1)}, u32[]{:S(2)}, u32[]{:S(2)}) async-start(bf16[8,2,32768]{2,1,0:T(2,128)(2,1)} %reshape.186), calls=%async_computation.2 | async-start | bytes 2097152 | tf_op jit(solution)/shard_map/all_to_all | solution.py:50
  96.3 3.1 reduce.2
  99.4 6.1 %reshape.185 = f32[2048,8,16]{2,1,0:T(8,128)} reshape(f32[8,32768]{1,0:T(8,128)S(1)} %reduce.2) | data formatting | bytes 2097152
  105.5 5.4 %copy.96 = f32[16,8,8,256]{3,2,1,0:T(8,128)S(1)} copy(f32[16,8,8,256]{0,2,3,1:T(8,128)} %bitcast.155) | data formatting | bytes 2097152 | tf_op jit(solution)/shard_map/all_to_all | solution.py:43
  112.4 9.5 %all-to-all-done.2 = bf16[8,2,32768]{2,1,0:T(2,128)(2,1)S(1)} async-done(((bf16[8,2,32768]{2,1,0:T(2,128)(2,1)}), bf16[8,2,32768]{2,1,0:T(2,128)(2,1)S(1)}, u32[]{:S(2)}, u32[]{:S(2)}) %all-to-all-start.2) | async-done | bytes 1048608 | tf_op jit(solution)/shard_map/all_to_all | solution.py:50
  121.9 7.6 %reshape.187 = bf16[2048,2,8,16]{3,2,1,0:T(8,128)(2,1)} reshape(bf16[8,2,32768]{2,1,0:T(2,128)(2,1)S(1)} %all-to-all-done.2) | data formatting | bytes 2097152
  129.5 8.9 %copy.104 = bf16[2,16,8,8,256]{4,2,3,1,0:T(8,128)(2,1)S(1)} copy(bf16[2,16,8,8,256]{1,2,0,4,3:T(8,128)(2,1)} %bitcast.156) | data formatting | bytes 2097152 | tf_op jit(solution)/shard_map/all_to_all | solution.py:50
  140.2 43.6 %all-reduce.1 = bf16[1024,160]{0,1:T(8,128)(2,1)} all-reduce(f32[1024,160]{0,1:T(8,128)S(1)} %fusion.29), channel_id=1, replica_groups=mesh['req'=8,'grp'=4] {'req'}, use_global_device_ids=true, to_apply=%region_1.2 | all-reduce | flops 163840 | bytes 983040 | tf_op jit(solution)/shard_map/psum | solution.py:67
  184.7 2.7 compare_select_fusion
  187.4 2.4 reshape.145
  191.2 132.7 %while.15 = (s32[]{:T(128)}, f32[16,16384]{1,0:T(8,128)S(1)}, f32[16,16384]{1,0:T(8,128)S(1)}, f32[16,16384]{1,0:T(8,128)}, f32[16,16384]{1,0:T(8,128)}, /*index...) while((s32[]{:T(128)}, f32[16,16384]{1,0:T(8,128)S(1)}, ...), condition=%wide.region_4.5_spmd.clone, body=%wide.region_2.4_spmd.clone.sunk | while | flops 1835075 | bytes 18522676 | solution.py:104
  192.9 1.3 constant_dynamic-slice_fusion.6
  197.6 1.9 dynamic_update_slice.6
  201.2 1.3 constant_dynamic-slice_fusion.6
  205.9 1.9 dynamic_update_slice.6
  209.5 1.3 constant_dynamic-slice_fusion.6
  214.2 1.9 dynamic_update_slice.6
  217.8 1.3 constant_dynamic-slice_fusion.6
  222.5 1.9 dynamic_update_slice.6
  226.1 1.3 constant_dynamic-slice_fusion.6
  230.7 1.9 dynamic_update_slice.6
  234.3 1.3 constant_dynamic-slice_fusion.6
  239.0 1.9 dynamic_update_slice.6
  242.6 1.3 constant_dynamic-slice_fusion.6
  247.3 1.9 dynamic_update_slice.6
  250.9 1.3 constant_dynamic-slice_fusion.6
  255.6 1.9 dynamic_update_slice.6
  259.2 1.3 constant_dynamic-slice_fusion.6
  263.9 1.9 dynamic_update_slice.6
  267.5 1.3 constant_dynamic-slice_fusion.6
  272.2 1.9 dynamic_update_slice.6
  275.8 1.3 constant_dynamic-slice_fusion.6
  280.5 1.9 dynamic_update_slice.6
  288.8 1.9 dynamic_update_slice.6
  292.4 1.3 constant_dynamic-slice_fusion.6
  297.1 1.9 dynamic_update_slice.6
  300.7 1.3 constant_dynamic-slice_fusion.6
  305.4 1.9 dynamic_update_slice.6
  313.7 1.9 dynamic_update_slice.6
  317.3 1.3 constant_dynamic-slice_fusion.6
  322.0 1.9 dynamic_update_slice.6
  323.9 1.5 copy.127
  325.5 1.5 fusion.16
  328.1 3.5 all-to-all-start.3
  332.7 9.4 %all-to-all-done.3 = bf16[16,64,256]{2,0,1:T(8,128)(2,1)S(1)} async-done(((bf16[16,64,256]{2,0,1:T(8,128)(2,1)}), bf16[16,64,256]{2,0,1:T(8,128)(2,1)S(1)}, u32[]{:S(2)}, u32[]{:S(2)}) %all-to-all-start.3) | async-done | bytes 524320 | tf_op jit(solution)/shard_map/all_to_all | solution.py:109
  342.1 9.1 %all-to-all-start.4 = ((f32[16,64,256]{2,0,1:T(8,128)}), f32[16,64,256]{2,0,1:T(8,128)S(1)}, u32[]{:S(2)}, u32[]{:S(2)}) async-start(f32[16,64,256]{2,0,1:T(8,128)} %bitcast.121), calls=%async_computation.4 | async-start | bytes 2097152 | tf_op jit(solution)/shard_map/all_to_all | solution.py:116
  351.6 2.9 fusion.2
  355.4 12.2 %all-to-all-done.4 = f32[16,64,256]{2,0,1:T(8,128)S(1)} async-done(((f32[16,64,256]{2,0,1:T(8,128)}), f32[16,64,256]{2,0,1:T(8,128)S(1)}, u32[]{:S(2)}, u32[]{:S(2)}) %all-to-all-start.4) | async-done | bytes 1048608 | tf_op jit(solution)/shard_map/all_to_all | solution.py:116
  368.2 1.6 copy.113
  (283 shorter events, 84.1 us)
Async XLA Ops:
  0.6 139.3 %copy-start = (bf16[256,160]{0,1:T(8,128)(2,1)S(1)}, bf16[256,160]{0,1:T(8,128)(2,1)}, u32[]{:S(2)}) copy-start(bf16[256,160]{0,1:T(8,128)(2,1)} %param.24) | copy-start | bytes 245764
  0.6 20.3 %copy-start.3 = (f32[8,16,2048]{2,1,0:T(8,128)S(1)}, f32[8,16,2048]{2,1,0:T(8,128)}, u32[]{:S(2)}) copy-start(f32[8,16,2048]{2,1,0:T(8,128)} %param.30) | copy-start | bytes 3145732
  8.6 17.1 %copy-start.2 = (bf16[8,16,1024]{2,1,0:T(8,128)(2,1)S(1)}, bf16[8,16,1024]{2,1,0:T(8,128)(2,1)}, u32[]{:S(2)}) copy-start(bf16[8,16,1024]{2,1,0:T(8,128)(2,1)} %param.19) | copy-start | bytes 786436
  8.6 17.4 %copy-start.4 = (f32[1024]{0:T(1024)S(1)}, f32[1024]{0:T(1024)}, u32[]{:S(2)}) copy-start(f32[1024]{0:T(1024)} %param.20) | copy-start | bytes 12292
  13.7 47.4 %all-to-all-start.1 = ((f32[8,1,6144]{2,1,0:T(1,128)}), f32[8,1,6144]{2,1,0:T(1,128)S(1)}, u32[]{:S(2)}, u32[]{:S(2)}) async-start(f32[8,1,6144]{2,1,0:T(1,128)} %reshape.188), calls=%async_computation.1 | async-start | bytes 393216 | tf_op jit(solution)/shard_map/all_to_all | solution.py:44
  52.9 8.2 %copy-start.12 = (s32[64]{0:T(128)S(1)}, s32[64]{0:T(128)}, u32[]{:S(2)}) copy-start(s32[64]{0:T(128)} %param.33) | copy-start | bytes 772
  52.9 14.3 %copy-start.13 = (s32[64]{0:T(128)S(1)}, s32[64]{0:T(128)}, u32[]{:S(2)}) copy-start(s32[64]{0:T(128)} %param.32) | copy-start | bytes 772
  52.9 25.7 %copy-start.9 = (s32[64]{0:T(128)S(1)}, s32[64]{0:T(128)}, u32[]{:S(2)}) copy-start(s32[64]{0:T(128)} %param.35) | copy-start | bytes 772
  52.9 25.9 %copy-start.6 = (f32[4,256]{1,0:T(4,128)S(1)}, f32[4,256]{1,0:T(4,128)}, u32[]{:S(2)}) copy-start(f32[4,256]{1,0:T(4,128)} %param.22) | copy-start | bytes 12292
  52.9 25.9 %copy-start.5 = (f32[16,256]{1,0:T(8,128)S(1)}, f32[16,256]{1,0:T(8,128)}, u32[]{:S(2)}) copy-start(f32[16,256]{1,0:T(8,128)} %param.27) | copy-start | bytes 49156
  61.1 31.4 %all-to-all-start = ((f32[8,1,32768]{2,1,0:T(1,128)}), f32[8,1,32768]{2,1,0:T(1,128)S(1)}, u32[]{:S(2)}, u32[]{:S(2)}) async-start(f32[8,1,32768]{2,1,0:T(1,128)} %reshape.184), calls=%async_computation | async-start | bytes 2097152 | tf_op jit(solution)/shard_map/all_to_all | solution.py:43
  92.5 29.4 %all-to-all-start.2 = ((bf16[8,2,32768]{2,1,0:T(2,128)(2,1)}), bf16[8,2,32768]{2,1,0:T(2,128)(2,1)S(1)}, u32[]{:S(2)}, u32[]{:S(2)}) async-start(bf16[8,2,32768]{2,1,0:T(2,128)(2,1)} %reshape.186), calls=%async_computation.2 | async-start | bytes 2097152 | tf_op jit(solution)/shard_map/all_to_all | solution.py:50
  112.4 27.0 %copy-start.7 = (f32[256]{0:T(256)S(1)}, f32[256]{0:T(256)}, u32[]{:S(2)}) copy-start(f32[256]{0:T(256)} %param.23) | copy-start | bytes 3076
  129.5 55.2 %copy-start.10 = (bf16[128,256]{1,0:T(8,128)(2,1)S(1)}, bf16[128,256]{1,0:T(8,128)(2,1)}, u32[]{:S(2)}) copy-start(bf16[128,256]{1,0:T(8,128)(2,1)} %param.25) | copy-start | bytes 196612
  129.5 55.2 %copy-start.11 = (f32[256]{0:T(256)S(1)}, f32[256]{0:T(256)}, u32[]{:S(2)}) copy-start(f32[256]{0:T(256)} %param.26) | copy-start | bytes 3076
  138.4 1.0 copy-start.1
  138.4 52.8 %copy-start.14 = (s32[64]{0:T(128)S(1)}, s32[64]{0:T(128)}, u32[]{:S(2)}) copy-start(s32[64]{0:T(128)} %param.34) | copy-start | bytes 772
  191.2 134.3 %copy-start.8 = (f32[256]{0:T(256)S(1)}, f32[256]{0:T(256)}, u32[]{:S(2)}) copy-start(f32[256]{0:T(256)} %param.28) | copy-start | bytes 3076
  328.1 14.0 %all-to-all-start.3 = ((bf16[16,64,256]{2,0,1:T(8,128)(2,1)}), bf16[16,64,256]{2,0,1:T(8,128)(2,1)S(1)}, u32[]{:S(2)}, u32[]{:S(2)}) async-start(bf16[16,64,256]{2,0,1:T(8,128)(2,1)} %copy.108), calls=%async_computation.3 | async-start | bytes 1048576 | tf_op jit(solution)/shard_map/all_to_all | solution.py:109
  342.1 25.5 %all-to-all-start.4 = ((f32[16,64,256]{2,0,1:T(8,128)}), f32[16,64,256]{2,0,1:T(8,128)S(1)}, u32[]{:S(2)}, u32[]{:S(2)}) async-start(f32[16,64,256]{2,0,1:T(8,128)} %bitcast.121), calls=%async_computation.4 | async-start | bytes 2097152 | tf_op jit(solution)/shard_map/all_to_all | solution.py:116
where the time goes:
time: 372 us; the launch traced here: 370 us
  local copies, waits for them, and re-layouts  191 us (51%)
  other arithmetic  47.8 us (13%)
  blocking collectives  43.6 us (12%)
  waiting for transfers between devices  33.9 us (9%)
  starting transfers between devices  29.5 us (8%)
  loops' own time  12.3 us (3%)
  matrix products  10.8 us (3%)
    unnamed x47, local copies, waits for them, and re-layouts  70.4 us
    psum x1, blocking collectives, on_device(): mixed_rows = lax.psum(partial_value, 'req').astype(jnp.bfloat16)  43.6 us
    dynamic_update_slice x16, local copies, waits for them, and re-layouts, on_device(): lax.scan(advance, (start_flat, start_flat), sliced)  31.1 us
    while x48, local copies, waits for them, and re-layouts  29.4 us
    dynamic_slice x16, other arithmetic, on_device(): lax.scan(advance, (start_flat, start_flat), sliced)  20.9 us
    reduce_sum x16, other arithmetic, advance(): result = jnp.sum(spread(step_c) * current, axis=0)  14.9 us
    another operation x1, loops' own time, on_device(): lax.scan(advance, (start_flat, start_flat), sliced)  12.3 us
    all_to_all x1, waiting for transfers between devices, on_device(): lax.all_to_all(chosen.reshape(state_size, all_reqs, channels), 'req', spl...  12.2 us
  transfers between devices with their start and end apart: 5, of which 4 were waited for; matrix products, arithmetic and copies ran while one was open for 23% of the time, Pallas kernels for 0%

commit v1 on v0

--- a/solution.py
+++ b/solution.py
@@ -4,6 +4,22 @@
 from jax.sharding import PartitionSpec as P
 
 EPS = 1e-05
+
+
+def pairwise_exchange(x, axis, split, join):
+    ways, here = (lax.axis_size(axis), lax.axis_index(axis))
+    width = x.shape[split] // ways
+    shape = list(x.shape)
+    shape[split] = width
+    height = shape[join]
+    shape[join] = height * ways
+    full = jnp.zeros(shape, x.dtype)
+    for mask in range(ways):
+        part = lax.dynamic_slice_in_dim(x, (here ^ mask) * width, width, axis=split)
+        if mask:
+            part = lax.ppermute(part, axis, [(d, d ^ mask) for d in range(ways)])
+        full = lax.dynamic_update_slice_in_dim(full, part, (here ^ mask) * height, axis=join)
+    return full
 
 
 def rms_normed(values_in, norm_gain):
@@ -47,7 +63,7 @@
     normed = rms_normed(token_major, norm_gain)
     projected = jnp.dot(normed, in_weight, preferred_element_type=jnp.float32).astype(jnp.bfloat16)
     projected = jnp.moveaxis(projected.reshape(draft_len, local_reqs, 2, inner_width), 2, 0)
-    grouped = lax.all_to_all(projected, "req", split_axis=3, concat_axis=2, tiled=True)
+    grouped = pairwise_exchange(projected, "req", 3, 2)
     all_reqs = grouped.shape[2]
     inner_part = grouped[0]
     gate_part = grouped[1]

time: 372 us -> 330 us (0.89)
  local copies, waits for them, and re-layouts: 191 us -> 142 us
  starting transfers between devices: 29.5 us -> 36.9 us
  waiting for transfers between devices: 33.9 us -> 29.8 us
  other arithmetic: 47.8 us -> 51.6 us
    unnamed x47 -> x51, local copies, waits for them, and re-layouts: 70.4 us -> 43.1 us
    ppermute x0 -> x7, starting transfers between devices: none -> 14.5 us  [pairwise_exchange(): part = lax.ppermute(part, axis, [(d, d ^ mask) for d in range(ways)])]
    all_to_all x1 -> x0, waiting for transfers between devices: 9.5 us -> none  [on_device(): lax.all_to_all(projected, 'req', split_axis=3, concat_axis=2, tiled=True)]
    all_to_all x1 -> x0, local copies, waits for them, and re-layouts: 8.9 us -> none  [on_device(): lax.all_to_all(projected, 'req', split_axis=3, concat_axis=2, tiled=True)]
    reshape x1 -> x0, local copies, waits for them, and re-layouts: 8.85 us -> none  [on_device(): projected.reshape(draft_len, local_reqs, 2, inner_width)]
    ppermute x0 -> x7, waiting for transfers between devices: none -> 6.18 us  [pairwise_exchange(): part = lax.ppermute(part, axis, [(d, d ^ mask) for d in range(ways)])]
    all_to_all x1 -> x0, starting transfers between devices: 3.74 us -> none  [on_device(): lax.all_to_all(projected, 'req', split_axis=3, concat_axis=2, tiled=True)]
  transfers between devices with their start and end apart: 5 -> 11, of which waited for: 4 -> 4; matrix products, arithmetic and copies ran while one was open for 23% -> 17% of each run, Pallas kernels for 0% -> 0%
where the time goes in v1:
time: 330 us; the launch traced here: 328 us
  local copies, waits for them, and re-layouts  142 us (43%)
  other arithmetic  51.6 us (16%)
  blocking collectives  45.6 us (14%)
  starting transfers between devices  36.9 us (11%)
  waiting for transfers between devices  29.8 us (9%)
  loops' own time  11.8 us (4%)
  matrix products  9.01 us (3%)
    psum x1, blocking collectives, on_device(): mixed_rows = lax.psum(partial_value, 'req').astype(jnp.bfloat16)  45.6 us
    unnamed x51, local copies, waits for them, and re-layouts  43.1 us
    dynamic_update_slice x16, local copies, waits for them, and re-layouts, on_device(): lax.scan(advance, (start_flat, start_flat), sliced)  31 us
    while x48, local copies, waits for them, and re-layouts  29.4 us
    dynamic_slice x16, other arithmetic, on_device(): lax.scan(advance, (start_flat, start_flat), sliced)  20.9 us
    reduce_sum x16, other arithmetic, advance(): result = jnp.sum(spread(step_c) * current, axis=0)  14.9 us
    ppermute x7, starting transfers between devices, pairwise_exchange(): part = lax.ppermute(part, axis, [(d, d ^ mask) for d in range(ways)])  14.5 us
    all_to_all x1, waiting for transfers between devices, on_device(): lax.all_to_all(chosen.reshape(state_size, all_reqs, channels), 'req', spl...  12.1 us
  transfers between devices with their start and end apart: 11, of which 4 were waited for; matrix products, arithmetic and copies ran while one was open for 17% of the time, Pallas kernels for 0%

profile of v1, /device:TPU:0, one launch (start us, length us, event | category | flops | bytes accessed | tf_op | source)
XLA Modules:
  0.0 328.4 jit_solution(14531337665926386724)
XLA Ops:
  2.0 4.9 %convolution_convert_fusion = bf16[128,4096]{1,0:T(8,128)(2,1)S(1)} fusion(bf16[1024,4096]{1,0:T(8,128)(2,1)} %param.21, f32[1024]{0:T(1024)} %param.20, f32[128]{0:T(128)S(1)} %rsqrt.12, bf16[8,16,1024]{2,1,0:T(8,128)(2,1)} %param.19), kind=kOutput, calls=%fused_computation.11 | convolution fusion | flops 1074790400 | bytes 9703936 | tf_op jit(solution)/shard_map/dot_general | solution.py:64
  7.1 3.0 collective-permute-start
  10.2 1.6 collective-permute-start.1
  11.9 3.1 collective-permute-start.3
  15.0 1.3 collective-permute-start.4
  16.3 2.7 copy.116
  19.1 3.9 %bitcast_bitcast_fusion.1 = f32[2048,3,8]{2,1,0:T(4,128)} fusion(f32[8,3,2048]{0,1,2:T(4,128)} %copy.116), kind=kLoop, calls=%fused_computation.95 | loop fusion | bytes 393216
  22.9 5.2 %reshape.182 = f32[8,1,6144]{2,1,0:T(1,128)} reshape(f32[2048,3,8]{2,1,0:T(4,128)} %bitcast_bitcast_fusion.1) | data formatting | bytes 393216
  28.1 4.9 %all-to-all-start.1 = ((f32[8,1,6144]{2,1,0:T(1,128)}), f32[8,1,6144]{2,1,0:T(1,128)S(1)}, u32[]{:S(2)}, u32[]{:S(2)}) async-start(f32[8,1,6144]{2,1,0:T(1,128)} %reshape.182), calls=%async_computation.1 | async-start | bytes 393216 | tf_op jit(solution)/shard_map/all_to_all | solution.py:60
  33.0 4.6 %copy.110 = f32[8,16,2048]{1,0,2:T(8,128)} copy(f32[8,16,2048]{2,1,0:T(8,128)S(1)} %copy-done.3) | data formatting | bytes 2097152 | tf_op args[11]
  37.7 5.8 %bitcast_bitcast_fusion = f32[2048,8,16]{2,1,0:T(8,128)} fusion(f32[8,16,2048]{1,0,2:T(8,128)} %copy.110), kind=kLoop, calls=%fused_computation.94 | loop fusion | bytes 2097152
  43.9 8.1 %reshape.180 = f32[8,1,32768]{2,1,0:T(1,128)} reshape(f32[2048,8,16]{2,1,0:T(8,128)} %bitcast_bitcast_fusion) | data formatting | bytes 2097152
  52.3 3.9 %collective-permute-start.5 = (bf16[2,16,8,256]{3,2,1,0:T(8,128)(2,1)S(1)}, bf16[2,16,8,256]{3,2,1,0:T(8,128)(2,1)S(1)}, u32[]{:S(2)}, u32[]{:S(2)}) collective-permute-start(bf16[2,16,8,256]{3,2,1,0:T(8,128)(2,1)S(1)} %bitcast.201), channel_id=1, source_target_pairs={{0,24},{4,28},{8,16},{12,20},{16,8},{20,12},{24,0},{28,4},{1,25},{... | collective-permute-start | bytes 393224 | tf_op jit(solution)/shard_map/ppermute | solution.py:20
  56.2 1.5 collective-permute-start.6
  57.9 1.4 collective-permute-done.5
  59.3 4.8 %collective-permute-done.6 = bf16[2,16,8,256]{3,2,1,0:T(8,128)(2,1)S(1)} collective-permute-done((bf16[2,16,8,256]{3,2,1,0:T(8,128)(2,1)S(1)}, bf16[2,16,8,256]{3,2,1,0:T(8,128)(2,1)S(1)}, u32[]{:S(2)}, u32[]{:S(2)}) %collective-permute-start.6) | collective-permute-done | bytes 131104 | tf_op jit(solution)/shard_map/ppermute | solution.py:20
  65.3 5.1 %all-to-all-start = ((f32[8,1,32768]{2,1,0:T(1,128)}), f32[8,1,32768]{2,1,0:T(1,128)S(1)}, u32[]{:S(2)}, u32[]{:S(2)}) async-start(f32[8,1,32768]{2,1,0:T(1,128)} %reshape.180), calls=%async_computation | async-start | bytes 2097152 | tf_op jit(solution)/shard_map/all_to_all | solution.py:59
  72.1 4.7 %reshape.183 = f32[2048,3,8]{2,1,0:T(4,128)} reshape(f32[8,6144]{1,0:T(8,128)S(1)} %reduce.3) | data formatting | bytes 393216
  76.8 3.5 %copy.117 = f32[3,8,8,256]{3,0,1,2:T(4,128)S(1)} copy(f32[3,8,8,256]{1,0,3,2:T(4,128)} %bitcast.174) | data formatting | bytes 393216 | tf_op jit(solution)/shard_map/all_to_all | solution.py:60
  81.3 3.0 multiply_convert_fusion
  84.6 45.6 %all-reduce.1 = bf16[1024,160]{0,1:T(8,128)(2,1)S(1)} all-reduce(f32[1024,160]{0,1:T(8,128)S(1)} %fusion.30), channel_id=1, replica_groups=mesh['req'=8,'grp'=4] {'req'}, use_global_device_ids=true, to_apply=%region_1.2 | all-reduce | flops 163840 | bytes 983040 | tf_op jit(solution)/shard_map/psum | solution.py:83
  133.6 3.1 reduce.2
  136.7 6.0 %reshape.181 = f32[2048,8,16]{2,1,0:T(8,128)} reshape(f32[8,32768]{1,0:T(8,128)S(1)} %reduce.2) | data formatting | bytes 2097152
  142.7 5.4 %copy.112 = f32[16,8,8,256]{3,2,1,0:T(8,128)S(1)} copy(f32[16,8,8,256]{0,2,3,1:T(8,128)} %bitcast.173) | data formatting | bytes 2097152 | tf_op jit(solution)/shard_map/all_to_all | solution.py:59
  149.7 130.9 %while.15 = (s32[]{:T(128)}, f32[16,16384]{1,0:T(8,128)S(1)}, f32[16,16384]{1,0:T(8,128)S(1)}, f32[16,16384]{1,0:T(8,128)}, f32[16,16384]{1,0:T(8,128)}, /*index...) while((s32[]{:T(128)}, f32[16,16384]{1,0:T(8,128)S(1)}, ...), condition=%wide.region_4.5_spmd.clone, body=%wide.region_2.4_spmd.clone.sunk | while | flops 1835075 | bytes 18522676 | solution.py:120
  151.6 1.3 constant_dynamic-slice_fusion.14
  156.2 1.9 dynamic_update_slice.46
  159.8 1.3 constant_dynamic-slice_fusion.14
  164.3 1.9 dynamic_update_slice.46
  167.9 1.3 constant_dynamic-slice_fusion.14
  172.5 1.9 dynamic_update_slice.46
  176.1 1.3 constant_dynamic-slice_fusion.14
  180.7 1.9 dynamic_update_slice.46
  184.2 1.3 constant_dynamic-slice_fusion.14
  188.8 1.9 dynamic_update_slice.46
  192.4 1.3 constant_dynamic-slice_fusion.14
  197.0 1.9 dynamic_update_slice.46
  200.6 1.3 constant_dynamic-slice_fusion.14
  205.1 1.9 dynamic_update_slice.46
  208.7 1.3 constant_dynamic-slice_fusion.14
  213.3 1.9 dynamic_update_slice.46
  216.9 1.3 constant_dynamic-slice_fusion.14
  221.4 2.0 dynamic_update_slice.46
  225.0 1.3 constant_dynamic-slice_fusion.14
  229.6 2.0 dynamic_update_slice.46
  233.2 1.3 constant_dynamic-slice_fusion.14
  237.8 2.0 dynamic_update_slice.46
  241.4 1.3 constant_dynamic-slice_fusion.14
  246.0 2.0 dynamic_update_slice.46
  249.6 1.3 constant_dynamic-slice_fusion.14
  254.1 2.0 dynamic_update_slice.46
  257.8 1.3 constant_dynamic-slice_fusion.14
  262.3 2.0 dynamic_update_slice.46
  265.9 1.3 constant_dynamic-slice_fusion.14
  270.5 2.0 dynamic_update_slice.46
  278.7 2.0 dynamic_update_slice.46
  280.6 1.5 copy.157
  282.2 1.5 fusion.16
  284.8 3.5 %all-to-all-start.2 = ((bf16[16,64,256]{2,0,1:T(8,128)(2,1)}), bf16[16,64,256]{2,0,1:T(8,128)(2,1)S(1)}, u32[]{:S(2)}, u32[]{:S(2)}) async-start(bf16[16,64,256]{2,0,1:T(8,128)(2,1)} %copy.130), calls=%async_computation.2 | async-start | bytes 1048576 | tf_op jit(solution)/shard_map/all_to_all | solution.py:125
  289.4 11.5 %all-to-all-done.2 = bf16[16,64,256]{2,0,1:T(8,128)(2,1)S(1)} async-done(((bf16[16,64,256]{2,0,1:T(8,128)(2,1)}), bf16[16,64,256]{2,0,1:T(8,128)(2,1)S(1)}, u32[]{:S(2)}, u32[]{:S(2)}) %all-to-all-start.2) | async-done | bytes 524320 | tf_op jit(solution)/shard_map/all_to_all | solution.py:125
  300.9 8.9 %all-to-all-start.3 = ((f32[16,64,256]{2,0,1:T(8,128)}), f32[16,64,256]{2,0,1:T(8,128)S(1)}, u32[]{:S(2)}, u32[]{:S(2)}) async-start(f32[16,64,256]{2,0,1:T(8,128)} %bitcast.132), calls=%async_computation.3 | async-start | bytes 2097152 | tf_op jit(solution)/shard_map/all_to_all | solution.py:132
  310.2 3.0 fusion.2
  314.1 12.1 %all-to-all-done.3 = f32[16,64,256]{2,0,1:T(8,128)S(1)} async-done(((f32[16,64,256]{2,0,1:T(8,128)}), f32[16,64,256]{2,0,1:T(8,128)S(1)}, u32[]{:S(2)}, u32[]{:S(2)}) %all-to-all-start.3) | async-done | bytes 1048608 | tf_op jit(solution)/shard_map/all_to_all | solution.py:132
  326.8 1.6 copy.135
  (306 shorter events, 84.0 us)
Async XLA Ops:
  0.6 83.6 %copy-start = (bf16[256,160]{0,1:T(8,128)(2,1)S(1)}, bf16[256,160]{0,1:T(8,128)(2,1)}, u32[]{:S(2)}) copy-start(bf16[256,160]{0,1:T(8,128)(2,1)} %param.24) | copy-start | bytes 245764
  2.0 14.3 %copy-start.4 = (bf16[8,3,2048]{2,0,1:T(8,128)(2,1)S(1)}, bf16[8,3,2048]{2,0,1:T(8,128)(2,1)}, u32[]{:S(2)}) copy-start(bf16[8,3,2048]{2,0,1:T(8,128)(2,1)} %param.31) | copy-start | bytes 294916
  7.1 45.2 %collective-permute-start = (bf16[2,16,8,256]{3,2,1,0:T(8,128)(2,1)S(1)}, bf16[2,16,8,256]{3,2,1,0:T(8,128)(2,1)S(1)}, u32[]{:S(2)}, u32[]{:S(2)}) collective-permute-start(bf16[2,16,8,256]{3,2,1,0:T(8,128)(2,1)S(1)} %bitcast.199), channel_id=1, source_target_pairs={{0,4},{4,0},{8,12},{12,8},{16,20},{20,16},{24,28},{28,24},{1,5},{5... | collective-permute-start | bytes 393224 | tf_op jit(solution)/shard_map/ppermute | solution.py:20
  10.2 46.1 %collective-permute-start.1 = (bf16[2,16,8,256]{3,2,1,0:T(8,128)(2,1)S(1)}, bf16[2,16,8,256]{3,2,1,0:T(8,128)(2,1)S(1)}, u32[]{:S(2)}, u32[]{:S(2)}) collective-permute-start(bf16[2,16,8,256]{3,2,1,0:T(8,128)(2,1)S(1)} %bitcast.198), channel_id=1, source_target_pairs={{0,8},{4,12},{8,0},{12,4},{16,24},{20,28},{24,16},{28,20},{1,9},{5... | collective-permute-start | bytes 393224 | tf_op jit(solution)/shard_map/ppermute | solution.py:20
  11.8 46.0 %collective-permute-start.2 = (bf16[2,16,8,256]{3,2,1,0:T(8,128)(2,1)S(1)}, bf16[2,16,8,256]{3,2,1,0:T(8,128)(2,1)S(1)}, u32[]{:S(2)}, u32[]{:S(2)}) collective-permute-start(bf16[2,16,8,256]{3,2,1,0:T(8,128)(2,1)S(1)} %bitcast.197), channel_id=1, source_target_pairs={{0,12},{4,8},{8,4},{12,0},{16,28},{20,24},{24,20},{28,16},{1,13},{... | collective-permute-start | bytes 393224 | tf_op jit(solution)/shard_map/ppermute | solution.py:20
  11.9 45.9 %collective-permute-start.3 = (bf16[2,16,8,256]{3,2,1,0:T(8,128)(2,1)S(1)}, bf16[2,16,8,256]{3,2,1,0:T(8,128)(2,1)S(1)}, u32[]{:S(2)}, u32[]{:S(2)}) collective-permute-start(bf16[2,16,8,256]{3,2,1,0:T(8,128)(2,1)S(1)} %bitcast.196), channel_id=1, source_target_pairs={{0,16},{4,20},{8,24},{12,28},{16,0},{20,4},{24,8},{28,12},{1,17},{... | collective-permute-start | bytes 393224 | tf_op jit(solution)/shard_map/ppermute | solution.py:20
  15.0 42.9 %collective-permute-start.4 = (bf16[2,16,8,256]{3,2,1,0:T(8,128)(2,1)S(1)}, bf16[2,16,8,256]{3,2,1,0:T(8,128)(2,1)S(1)}, u32[]{:S(2)}, u32[]{:S(2)}) collective-permute-start(bf16[2,16,8,256]{3,2,1,0:T(8,128)(2,1)S(1)} %bitcast.195), channel_id=1, source_target_pairs={{0,20},{4,16},{8,28},{12,24},{16,4},{20,0},{24,12},{28,8},{1,21},{... | collective-permute-start | bytes 393224 | tf_op jit(solution)/shard_map/ppermute | solution.py:20
  22.9 10.1 %copy-start.3 = (f32[8,16,2048]{2,1,0:T(8,128)S(1)}, f32[8,16,2048]{2,1,0:T(8,128)}, u32[]{:S(2)}) copy-start(f32[8,16,2048]{2,1,0:T(8,128)} %param.30) | copy-start | bytes 3145732
  28.1 37.2 %all-to-all-start.1 = ((f32[8,1,6144]{2,1,0:T(1,128)}), f32[8,1,6144]{2,1,0:T(1,128)S(1)}, u32[]{:S(2)}, u32[]{:S(2)}) async-start(f32[8,1,6144]{2,1,0:T(1,128)} %reshape.182), calls=%async_computation.1 | async-start | bytes 393216 | tf_op jit(solution)/shard_map/all_to_all | solution.py:60
  37.7 5.8 %copy-start.9 = (s32[64]{0:T(128)S(1)}, s32[64]{0:T(128)}, u32[]{:S(2)}) copy-start(s32[64]{0:T(128)} %param.33) | copy-start | bytes 772
  37.7 5.9 %copy-start.11 = (s32[64]{0:T(128)S(1)}, s32[64]{0:T(128)}, u32[]{:S(2)}) copy-start(s32[64]{0:T(128)} %param.32) | copy-start | bytes 772
  37.7 5.9 %copy-start.6 = (f32[4,256]{1,0:T(4,128)S(1)}, f32[4,256]{1,0:T(4,128)}, u32[]{:S(2)}) copy-start(f32[4,256]{1,0:T(4,128)} %param.22) | copy-start | bytes 12292
  37.7 5.9 %copy-start.5 = (f32[16,256]{1,0:T(8,128)S(1)}, f32[16,256]{1,0:T(8,128)}, u32[]{:S(2)}) copy-start(f32[16,256]{1,0:T(8,128)} %param.27) | copy-start | bytes 49156
  37.7 6.1 %copy-start.10 = (s32[64]{0:T(128)S(1)}, s32[64]{0:T(128)}, u32[]{:S(2)}) copy-start(s32[64]{0:T(128)} %param.35) | copy-start | bytes 772
  52.3 6.9 %collective-permute-start.5 = (bf16[2,16,8,256]{3,2,1,0:T(8,128)(2,1)S(1)}, bf16[2,16,8,256]{3,2,1,0:T(8,128)(2,1)S(1)}, u32[]{:S(2)}, u32[]{:S(2)}) collective-permute-start(bf16[2,16,8,256]{3,2,1,0:T(8,128)(2,1)S(1)} %bitcast.201), channel_id=1, source_target_pairs={{0,24},{4,28},{8,16},{12,20},{16,8},{20,12},{24,0},{28,4},{1,25},{... | collective-permute-start | bytes 393224 | tf_op jit(solution)/shard_map/ppermute | solution.py:20
  56.2 7.8 %collective-permute-start.6 = (bf16[2,16,8,256]{3,2,1,0:T(8,128)(2,1)S(1)}, bf16[2,16,8,256]{3,2,1,0:T(8,128)(2,1)S(1)}, u32[]{:S(2)}, u32[]{:S(2)}) collective-permute-start(bf16[2,16,8,256]{3,2,1,0:T(8,128)(2,1)S(1)} %bitcast.200), channel_id=1, source_target_pairs={{0,28},{4,24},{8,20},{12,16},{16,12},{20,8},{24,4},{28,0},{1,29},{... | collective-permute-start | bytes 393224 | tf_op jit(solution)/shard_map/ppermute | solution.py:20
  64.1 12.7 %copy-start.2 = (bf16[2,16,64,256]{3,2,1,0:T(8,128)(2,1)}, bf16[2,16,64,256]{3,2,1,0:T(8,128)(2,1)S(1)}, u32[]{:S(2)}) copy-start(bf16[2,16,64,256]{3,2,1,0:T(8,128)(2,1)S(1)} %constant_dynamic-update-slice_fusion) | copy-start | bytes 3145732
  65.3 68.2 %all-to-all-start = ((f32[8,1,32768]{2,1,0:T(1,128)}), f32[8,1,32768]{2,1,0:T(1,128)S(1)}, u32[]{:S(2)}, u32[]{:S(2)}) async-start(f32[8,1,32768]{2,1,0:T(1,128)} %reshape.180), calls=%async_computation | async-start | bytes 2097152 | tf_op jit(solution)/shard_map/all_to_all | solution.py:59
  72.1 9.2 %copy-start.7 = (f32[256]{0:T(256)S(1)}, f32[256]{0:T(256)}, u32[]{:S(2)}) copy-start(f32[256]{0:T(256)} %param.23) | copy-start | bytes 3076
  76.8 53.4 %copy-start.12 = (bf16[128,256]{1,0:T(8,128)(2,1)S(1)}, bf16[128,256]{1,0:T(8,128)(2,1)}, u32[]{:S(2)}) copy-start(bf16[128,256]{1,0:T(8,128)(2,1)} %param.25) | copy-start | bytes 196612
  76.8 53.4 %copy-start.13 = (f32[256]{0:T(256)S(1)}, f32[256]{0:T(256)}, u32[]{:S(2)}) copy-start(f32[256]{0:T(256)} %param.26) | copy-start | bytes 3076
  148.7 1.0 copy-start.14
  149.7 132.5 %copy-start.8 = (f32[256]{0:T(256)S(1)}, f32[256]{0:T(256)}, u32[]{:S(2)}) copy-start(f32[256]{0:T(256)} %param.28) | copy-start | bytes 3076
  284.8 16.1 %all-to-all-start.2 = ((bf16[16,64,256]{2,0,1:T(8,128)(2,1)}), bf16[16,64,256]{2,0,1:T(8,128)(2,1)S(1)}, u32[]{:S(2)}, u32[]{:S(2)}) async-start(bf16[16,64,256]{2,0,1:T(8,128)(2,1)} %copy.130), calls=%async_computation.2 | async-start | bytes 1048576 | tf_op jit(solution)/shard_map/all_to_all | solution.py:125
  300.9 25.3 %all-to-all-start.3 = ((f32[16,64,256]{2,0,1:T(8,128)}), f32[16,64,256]{2,0,1:T(8,128)S(1)}, u32[]{:S(2)}, u32[]{:S(2)}) async-start(f32[16,64,256]{2,0,1:T(8,128)} %bitcast.132), calls=%async_computation.3 | async-start | bytes 2097152 | tf_op jit(solution)/shard_map/all_to_all | solution.py:132
  310.2 18.2 %copy-start.1 = (bf16[256,160]{0,1:T(8,128)(2,1)S(1)}, bf16[256,160]{0,1:T(8,128)(2,1)}, u32[]{:S(2)}) copy-start(bf16[256,160]{0,1:T(8,128)(2,1)} %param.24) | copy-start | bytes 245764
